TPU v7x, 32 devices: a whole 2x2x4 slice. The times are simulated.
32 devices in a mesh: fiber: 16 (over z, y, core), freq: 2 (over x).
Axes of the slice: x: 2, y: 2, z: 4, core: 2. Of those that a mesh axis runs over, the one named last changes fastest.
Arguments:
- spectra: bfloat16 [2, 512, 16, 2048], P(None, 'freq', 'fiber'), may hold values from -128 to 128
- valid_mask: int32 [16, 2048], P('fiber'), may hold values 0 or 1
- pair_reach: int32 [16], replicated, may hold values from 1 to 2, as said below
Outputs:
- correlations: float32 [16, 5, 2, 128, 128], P('fiber', None, 'freq')
Inputs may be any that keep to these rules, and one draw needn't show every extreme that they name: Block b is paired with blocks b + 1 to b + pair_reach[b]; every draw holds some block with reach 1 and some with reach 2.
All inputs are finite; a program needn't handle non-finite values. No bound on the sum of `valid_mask` on one device may be relied on, other than what follows from the above.
Results may differ from a plain program's by a relative error of at most 0.0012.
Values may be sent and summed in bfloat16 or wider, within the bound.
A program may use at most 128 MiB of HBM per device.

v0:
```python
import jax
import jax.numpy as jnp
from jax import lax
from jax.sharding import PartitionSpec as P

FREQS = 512
BAND = 2
LAG_DEV = 1
first_bin = 64.0
lag_step = 24.0
transform_length = 2048.0


def shifted(block, axis, distance):
    devices = range(lax.axis_size(axis))
    route = [(i - distance, i) for i in devices if i - distance in devices]
    return lax.ppermute(block, axis, route)


def twiddles(bins, lag_count):
    lag_values = jnp.arange(lag_count, dtype=jnp.float32) * lag_step
    angle = 2.0 * jnp.pi / transform_length * lag_values[:, None] * (first_bin + bins)[None, :]
    paired = jnp.stack([jnp.cos(angle), -jnp.sin(angle)], axis=2)
    return paired.reshape(lag_count, 2 * bins.shape[0])


def left_form(block_data):
    upper_half = jnp.concatenate([block_data[0], block_data[1]], axis=1)
    lower_half = jnp.concatenate([block_data[1], -block_data[0]], axis=1)
    return jnp.stack([upper_half, lower_half], axis=1)


def right_form(block_data):
    return jnp.concatenate([block_data[0], block_data[1]], axis=1)


def correlate(left_side, right_side, factors):
    products = jnp.einsum(
        "fkwi,fwj->fkij", left_side, right_side, preferred_element_type=jnp.float32
    )
    flattened = products.reshape(2 * products.shape[0], -1)
    return jnp.dot(factors, flattened, precision=lax.Precision.HIGHEST)


def select_entry(table, position):
    positions = jnp.arange(table.shape[0], dtype=jnp.int32)
    return jnp.sum(jnp.where(positions == position, table, 0))


def spectra_from(block_data, offset):
    return shifted(block_data, "fiber", offset)


def result_from(lag_tile, offset):
    return shifted(lag_tile, "fiber", offset)


def shards(spectra, valid_mask, pair_reach):
    groups = lax.axis_size("freq")
    fibers = lax.axis_size("fiber")
    lag_count = LAG_DEV * groups
    masked = spectra * valid_mask.astype(jnp.bfloat16)
    raw_blocks = lax.all_to_all(masked, "fiber", split_axis=3, concat_axis=2, tiled=True)
    values = raw_blocks.astype(jnp.float32)
    energy = (
        lax.psum(jnp.sum(values[0] * values[0] + values[1] * values[1], axis=0), "freq") / FREQS
    )
    resident = (values / jnp.sqrt(energy + 1e-06)).astype(jnp.bfloat16)
    location = lax.axis_index("fiber")
    bin_count = resident.shape[1]
    bins = lax.axis_index("freq") * bin_count + jnp.arange(bin_count, dtype=jnp.int32)
    factors = twiddles(bins.astype(jnp.float32), lag_count)
    block = resident.shape[3]
    own_left = left_form(resident)

    def nothing(left_side, right_side, table_part):
        return jnp.zeros((lag_count, block * block), jnp.float32)

    partials = []
    for offset in range(BAND + 1):
        other = resident if offset == 0 else spectra_from(resident, -offset)
        usable = jnp.logical_and(
            offset <= select_entry(pair_reach, location), location + offset < fibers
        )
        partials.append(lax.cond(usable, correlate, nothing, own_left, right_form(other), factors))
    summed = lax.psum_scatter(jnp.stack(partials), "freq", scatter_dimension=1, tiled=True)
    forward = [summed[0]]
    backward = []
    for offset in range(1, BAND + 1):
        forward.append(summed[offset])
        backward.append(result_from(summed[offset], offset))
    tiles = []
    for lag_tile in backward[::-1]:
        shaped = lag_tile.reshape(lag_tile.shape[0], block, block)
        tiles.append(jnp.swapaxes(shaped, 1, 2))
    for lag_tile in forward:
        tiles.append(lag_tile.reshape(lag_tile.shape[0], block, block))
    return jnp.stack(tiles)[None]


def solution(mesh):
    return jax.shard_map(
        shards,
        mesh=mesh,
        in_specs=(P(None, "freq", "fiber", None), P("fiber", None), P()),
        out_specs=P("fiber", None, "freq", None, None),
        check_vma=False,
    )
```

profile of v0, /device:TPU:8, one launch (start us, length us, event | category | flops | bytes accessed | tf_op | source)
XLA Modules:
  0.0 357.9 jit_solution(4956096219900850626)
XLA Ops:
  6.5 4.8 %copy.69 = bf16[2,256,1,2048]{1,0,2,3:T(2,128)(2,1)S(1)} copy(bf16[2,256,1,2048]{3,1,2,0:T(8,128)(2,1)} %param.9) | data formatting | bytes 4194304 | tf_op args[0]
  11.4 6.9 %broadcast_multiply_fusion = bf16[2,256,1,2048]{1,0,2,3:T(2,128)(2,1)S(1)} fusion(bf16[2,256,1,2048]{1,0,2,3:T(2,128)(2,1)S(1)} %copy.69, bf16[2048]{0:T(1024)(128)(2,1)S(1)} %convert_reduce_fusion), kind=kLoop, calls=%fused_computation.23 | loop fusion | flops 1048576 | bytes 4198400 | tf_op jit(solution)/shard_map/mul | solution.py:62
  18.3 53.3 %all_to_all.4 = bf16[2,256,1,2048]{1,0,2,3:T(2,128)(2,1)S(1)} all-to-all(bf16[2,256,1,2048]{1,0,2,3:T(2,128)(2,1)S(1)} %broadcast_multiply_fusion), channel_id=1, replica_groups=mesh['fiber'=16,'freq'=2] {'fiber'}, dimensions={3} | all-to-all | bytes 4194304 | tf_op jit(solution)/shard_map/all_to_all | solution.py:63
  72.3 1.6 copy-done
  73.9 5.0 %psum.7 = f32[16,128]{1,0:T(8,128)S(1)} all-reduce(f32[16,128]{1,0:T(8,128)S(1)} %bitcast.99), channel_id=1, replica_groups=mesh['fiber'=16,'freq'=2] {'freq'}, use_global_device_ids=true, to_apply=%region_2.3 | all-reduce | flops 2048 | bytes 16384 | tf_op jit(solution)/shard_map/psum | solution.py:66
  78.9 4.0 %divide_convert_fusion = bf16[2,256,16,128]{1,3,2,0:T(8,128)(2,1)} fusion(f32[2,256,16,128]{1,3,2,0:T(8,128)} %bitcast.87, f32[16,128]{1,0:T(8,128)S(1)} %add_sqrt_fusion), kind=kLoop, calls=%fused_computation.13 | loop fusion | flops 2097152 | bytes 6299648 | tf_op jit(solution)/shard_map/convert_element_type | solution.py:68
  82.9 2.4 collective-permute-start
  85.3 2.7 collective-permute-start.1
  92.4 1.8 slice_bitcast_fusion.5
  94.6 2.4 pad_maximum_fusion
  97.1 70.2 %conditional.3 = (f32[1,2,16384]{2,1,0:T(2,128)S(1)}) conditional(s32[]{:T(128)} %convert_element_type.28, () %tuple.29, (bf16[256,2,32,128]{0,3,2,1:T(8,128)(2,1)}, bf16[256,32,128]{0,2,1:T(8,128)(2,1)S(1)}, f32[2,512]{1,0:T(2,128)S(1)}) %tuple.30), branch_computations={%region_3.4_spmd, %region_4.5_spmd} | conditional | flops 738197504 | bytes 94507048 | solution.py:85
  97.1 8.3 %copy.72 = bf16[256,2,32,128]{3,2,1,0:T(8,128)(2,1)} copy(bf16[256,2,32,128]{0,3,2,1:T(8,128)(2,1)} %get-tuple-element.107) | data formatting | bytes 8388608 | tf_op jit(solution)/shard_map
  105.4 3.4 copy.82
  108.8 14.7 %fusion.24 = f32[256,2,128,128]{3,2,1,0:T(8,128)} fusion(bf16[256,2,32,128]{3,2,1,0:T(8,128)(2,1)} %copy.72, bf16[256,32,128,1]{2,1,3,0:T(8,128)(2,1)S(1)} %copy.82), kind=kOutput, calls=%fused_computation.51 | convolution fusion | flops 536870912 | bytes 39845888 | tf_op jit(solution)/shard_map/cond/branch_1_fun/fkwi,fwj->fkij/dot_general | solution.py:38
  123.6 43.1 %fusion.3 = f32[1,2,16384]{2,1,0:T(2,128)S(1)} fusion(f32[2,512]{1,0:T(2,128)S(1)} %get-tuple-element.37, f32[64,8,128,128]{3,2,1,0:T(8,128)} %bitcast.84), kind=kOutput, calls=%fused_computation.3 | convolution fusion | flops 201326592 | bytes 33689600 | tf_op jit(solution)/shard_map/cond/branch_1_fun/dot_general | solution.py:42
  167.2 1.8 slice_bitcast_fusion.3
  169.2 1.8 slice_bitcast_fusion.1
  172.5 69.6 %conditional.4 = (f32[1,2,16384]{2,1,0:T(2,128)S(1)}) conditional(s32[]{:T(128)} %convert_element_type.34, () %tuple.31, (bf16[256,2,32,128]{0,3,2,1:T(8,128)(2,1)}, bf16[256,32,128]{0,2,1:T(8,128)(2,1)S(1)}, f32[2,512]{1,0:T(2,128)S(1)}) %tuple.32), branch_computations={%region_5.6_spmd, %region_6.7_spmd} | conditional | flops 738197504 | bytes 94507048 | solution.py:85
  172.5 8.3 %copy.74 = bf16[256,2,32,128]{3,2,1,0:T(8,128)(2,1)} copy(bf16[256,2,32,128]{0,3,2,1:T(8,128)(2,1)} %get-tuple-element.110) | data formatting | bytes 8388608 | tf_op jit(solution)/shard_map
  180.8 3.4 copy.83
  184.3 14.7 %fusion.25 = f32[256,2,128,128]{3,2,1,0:T(8,128)} fusion(bf16[256,2,32,128]{3,2,1,0:T(8,128)(2,1)} %copy.74, bf16[256,32,128,1]{2,1,3,0:T(8,128)(2,1)S(1)} %copy.83), kind=kOutput, calls=%fused_computation.52 | convolution fusion | flops 536870912 | bytes 39845888 | tf_op jit(solution)/shard_map/cond/branch_1_fun/fkwi,fwj->fkij/dot_general | solution.py:38
  199.0 42.9 %fusion.9 = f32[1,2,16384]{2,1,0:T(2,128)S(1)} fusion(f32[2,512]{1,0:T(2,128)S(1)} %get-tuple-element.40, f32[64,8,128,128]{3,2,1,0:T(8,128)} %bitcast.85), kind=kOutput, calls=%fused_computation.7 | convolution fusion | flops 201326592 | bytes 33689600 | tf_op jit(solution)/shard_map/cond/branch_1_fun/dot_general | solution.py:42
  242.1 69.4 %conditional.5 = (f32[1,2,16384]{2,1,0:T(2,128)S(1)}) conditional(s32[]{:T(128)} %convert_element_type.35, () %tuple.33, (bf16[256,2,32,128]{0,3,2,1:T(8,128)(2,1)}, bf16[256,32,128]{0,2,1:T(8,128)(2,1)}, f32[2,512]{1,0:T(2,128)S(1)}) %tuple.34), branch_computations={%region_7.8_spmd, %region_8.9_spmd} | conditional | flops 738197504 | bytes 86118408 | solution.py:85
  242.2 8.0 %copy.76 = bf16[256,2,32,128]{3,2,1,0:T(8,128)(2,1)} copy(bf16[256,2,32,128]{0,3,2,1:T(8,128)(2,1)} %get-tuple-element.113) | data formatting | bytes 8388608 | tf_op jit(solution)/shard_map
  250.1 3.4 copy.84
  253.6 14.7 %fusion.26 = f32[256,2,128,128]{3,2,1,0:T(8,128)} fusion(bf16[256,2,32,128]{3,2,1,0:T(8,128)(2,1)} %copy.76, bf16[256,32,128,1]{2,1,3,0:T(8,128)(2,1)S(1)} %copy.84), kind=kOutput, calls=%fused_computation.53 | convolution fusion | flops 536870912 | bytes 39845888 | tf_op jit(solution)/shard_map/cond/branch_1_fun/fkwi,fwj->fkij/dot_general | solution.py:38
  268.3 43.0 %fusion.15 = f32[1,2,16384]{2,1,0:T(2,128)S(1)} fusion(f32[2,512]{1,0:T(2,128)S(1)} %get-tuple-element.43, f32[64,8,128,128]{3,2,1,0:T(8,128)} %bitcast.86), kind=kOutput, calls=%fused_computation.11 | convolution fusion | flops 201326592 | bytes 33689600 | tf_op jit(solution)/shard_map/cond/branch_1_fun/dot_general | solution.py:42
  313.1 25.0 %all-reduce.3.cloned.1.call-done = f32[3,2,16384]{2,1,0:T(2,128)} async-done(((f32[3,2,16384]{2,1,0:T(2,128)}), f32[3,2,16384]{2,1,0:T(2,128)}) %all-reduce.3.cloned.1.call-update) | async-done | bytes 393232
  338.1 1.9 constant_dynamic-slice_fusion.2
  339.9 3.4 collective-permute-start.2
  343.3 1.9 collective-permute-start.3
  347.0 2.8 collective-permute-done.3
  (42 shorter events, 9.5 us)
Async XLA Ops:
  6.5 4.8 %copy-start.3 = (s32[1,2048]{1,0:T(1,128)S(1)}, s32[1,2048]{1,0:T(1,128)}, u32[]{:S(2)}) copy-start(s32[1,2048]{1,0:T(1,128)} %param.10) | copy-start | bytes 24580
  6.5 331.5 %all-reduce.3.cloned.1.call-start = ((), (), s32[]{:S(2)}) async-start(), calls=%async_computation.1 | async-start | bytes 786432
  72.0 1.9 copy-start
  78.9 9.1 %copy-start.4 = (s32[16]{0:T(128)S(1)}, s32[16]{0:T(128)}, u32[]{:S(2)}) copy-start(s32[16]{0:T(128)} %param.11) | copy-start | bytes 196
  82.9 84.4 %collective-permute-start = (bf16[2,256,16,128]{1,3,2,0:T(8,128)(2,1)}, bf16[2,256,16,128]{1,3,2,0:T(8,128)(2,1)}, u32[]{:S(2)}, u32[]{:S(2)}) collective-permute-start(bf16[2,256,16,128]{1,3,2,0:T(8,128)(2,1)} %divide_convert_fusion), channel_id=1, source_target_pairs={{2,0},{4,2},{6,4},{8,6},{10,8},{12,10},{14,12},{16,14},{18,16},{20... | collective-permute-start | bytes 6291464 | tf_op jit(solution)/shard_map/ppermute | solution.py:17
  85.3 83.9 %collective-permute-start.1 = (bf16[2,256,16,128]{1,3,2,0:T(8,128)(2,1)}, bf16[2,256,16,128]{1,3,2,0:T(8,128)(2,1)}, u32[]{:S(2)}, u32[]{:S(2)}) collective-permute-start(bf16[2,256,16,128]{1,3,2,0:T(8,128)(2,1)} %divide_convert_fusion), channel_id=1, source_target_pairs={{4,0},{6,2},{8,4},{10,6},{12,8},{14,10},{16,12},{18,14},{20,16},{2... | collective-permute-start | bytes 6291464 | tf_op jit(solution)/shard_map/ppermute | solution.py:17
  97.1 8.3 %copy-start.2 = (bf16[256,32,128]{0,2,1:T(8,128)(2,1)}, bf16[256,32,128]{0,2,1:T(8,128)(2,1)S(1)}, u32[]{:S(2)}) copy-start(bf16[256,32,128]{0,2,1:T(8,128)(2,1)S(1)} %get-tuple-element.108) | copy-start | bytes 6291460 | tf_op jit(solution)/shard_map/cond
  172.5 8.3 %copy-start.1 = (bf16[256,32,128]{0,2,1:T(8,128)(2,1)}, bf16[256,32,128]{0,2,1:T(8,128)(2,1)S(1)}, u32[]{:S(2)}) copy-start(bf16[256,32,128]{0,2,1:T(8,128)(2,1)S(1)} %get-tuple-element.111) | copy-start | bytes 6291460 | tf_op jit(solution)/shard_map/cond
  242.1 70.4 %copy-start.5 = (u32[32]{0:T(128)S(1)}, u32[32]{0:T(128)}, u32[]{:S(2)}) copy-start(u32[32]{0:T(128)} %constant.41) | copy-start | bytes 388
  339.9 7.1 %collective-permute-start.2 = (f32[1,16384]{1,0:T(1,128)S(1)}, f32[1,16384]{1,0:T(1,128)S(1)}, u32[]{:S(2)}, u32[]{:S(2)}) collective-permute-start(f32[1,16384]{1,0:T(1,128)S(1)} %bitcast.94), channel_id=1, source_target_pairs={{0,4},{2,6},{4,8},{6,10},{8,12},{10,14},{12,16},{14,18},{16,20},{1... | collective-permute-start | bytes 196616 | tf_op jit(solution)/shard_map/ppermute | solution.py:17
  343.3 6.5 %collective-permute-start.3 = (f32[1,16384]{1,0:T(1,128)S(1)}, f32[1,16384]{1,0:T(1,128)S(1)}, u32[]{:S(2)}, u32[]{:S(2)}) collective-permute-start(f32[1,16384]{1,0:T(1,128)S(1)} %bitcast.92), channel_id=1, source_target_pairs={{0,2},{2,4},{4,6},{6,8},{8,10},{10,12},{12,14},{14,16},{16,18},{18... | collective-permute-start | bytes 196616 | tf_op jit(solution)/shard_map/ppermute | solution.py:17
Sparse Core Ops, SparseCore 0:
  312.6 25.3 all-reduce.2
where the time goes:
time: 365 us; the launch traced here: 358 us
  matrix products  173 us (47%)
  blocking collectives  58.2 us (16%)
  local copies, waits for them, and re-layouts  50.6 us (14%)
  waiting for transfers between devices  29.2 us (8%)
  other arithmetic  19.2 us (5%)
  between operations  16 us (4%)
  starting transfers between devices  10.4 us (3%)
    dot_general x3, matrix products, correlate(): return jnp.dot(factors, flattened, precision=lax.Precision.HIGHEST)  129 us
    all_to_all x1, blocking collectives, shards(): lax.all_to_all(masked, 'fiber', split_axis=3, concat_axis=2, tiled=True)  53.3 us
    dot_general x3, matrix products, correlate(): jnp.einsum('fkwi,fwj->fkij', left_side, right_side, preferred_element_typ...  44.1 us
    another operation x6, local copies, waits for them, and re-layouts  34.9 us
    unnamed x2, waiting for transfers between devices  25 us
    ppermute x4, starting transfers between devices, shifted(): return lax.ppermute(block, axis, route)  10.4 us
  transfers between devices with their start and end apart: 5, of which 3 were waited for; matrix products, arithmetic and copies ran while one was open for 22% of the time, Pallas kernels for 0%

commit v1 on v0

--- a/solution.py
+++ b/solution.py
@@ -60,7 +60,10 @@
     fibers = lax.axis_size("fiber")
     lag_count = LAG_DEV * groups
     masked = spectra * valid_mask.astype(jnp.bfloat16)
-    raw_blocks = lax.all_to_all(masked, "fiber", split_axis=3, concat_axis=2, tiled=True)
+    size = lax.axis_size("fiber")
+    blocks = jnp.stack(jnp.split(masked, size, axis=3), axis=0)
+    blocks = lax.all_to_all(blocks, "fiber", split_axis=0, concat_axis=0)
+    raw_blocks = jnp.concatenate(blocks, axis=2)
     values = raw_blocks.astype(jnp.float32)
     energy = (
         lax.psum(jnp.sum(values[0] * values[0] + values[1] * values[1], axis=0), "freq") / FREQS

time: 365 us -> 321 us (0.88)
  local copies, waits for them, and re-layouts: 50.6 us -> 10.1 us
  other arithmetic: 19.2 us -> 12.8 us
  matrix products: 173 us -> 177 us
    another operation x6 -> x1, local copies, waits for them, and re-layouts: 34.9 us -> 0.05 us  [shards(): blocks = jnp.stack(jnp.split(masked, size, axis=3), axis=0)]
    unnamed x14 -> x24, local copies, waits for them, and re-layouts: 7.04 us -> 1.38 us
    mul x1, other arithmetic: 6.92 us -> 1.73 us  [shards(): masked = spectra * valid_mask.astype(jnp.bfloat16)]
    dot_general x3, matrix products: 44.1 us -> 48 us  [correlate(): jnp.einsum('fkwi,fwj->fkij', left_side, right_side, preferred_element_typ...]
where the time goes in v1:
time: 321 us; the launch traced here: 315 us
  matrix products  177 us (55%)
  blocking collectives  58.3 us (18%)
  waiting for transfers between devices  29.2 us (9%)
  between operations  16 us (5%)
  other arithmetic  12.8 us (4%)
  starting transfers between devices  10.4 us (3%)
  local copies, waits for them, and re-layouts  10.1 us (3%)
    dot_general x3, matrix products, correlate(): return jnp.dot(factors, flattened, precision=lax.Precision.HIGHEST)  129 us
    all_to_all x1, blocking collectives, shards(): blocks = lax.all_to_all(blocks, 'fiber', split_axis=0, concat_axis=0)  53.3 us
    dot_general x3, matrix products, correlate(): jnp.einsum('fkwi,fwj->fkij', left_side, right_side, preferred_element_typ...  48 us
    unnamed x2, waiting for transfers between devices  25 us
    ppermute x4, starting transfers between devices, shifted(): return lax.ppermute(block, axis, route)  10.4 us
  transfers between devices with their start and end apart: 5, of which 3 were waited for; matrix products, arithmetic and copies ran while one was open for 22% of the time, Pallas kernels for 0%

profile of v1, /device:TPU:8, one launch (start us, length us, event | category | flops | bytes accessed | tf_op | source)
XLA Modules:
  0.0 315.0 jit_solution(11742878786791450981)
XLA Ops:
  6.5 0.7 convert_reduce_fusion
  7.3 1.7 bitcast_multiply_fusion
  9.8 53.3 %all_to_all.5 = bf16[16,2,256,1,128]{4,2,1,3,0:T(8,128)(2,1)S(1)} all-to-all(bf16[16,2,256,1,128]{4,2,1,3,0:T(8,128)(2,1)S(1)} %fusion.31), channel_id=1, replica_groups=mesh['fiber'=16,'freq'=2] {'fiber'}, dimensions={0} | all-to-all | bytes 4194304 | tf_op jit(solution)/shard_map/all_to_all | solution.py:65
  63.9 5.0 %psum.7 = f32[16,128]{1,0:T(8,128)S(1)} all-reduce(f32[16,128]{1,0:T(8,128)S(1)} %fusion.30), channel_id=1, replica_groups=mesh['fiber'=16,'freq'=2] {'freq'}, use_global_device_ids=true, to_apply=%region_2.3 | all-reduce | flops 2048 | bytes 16384 | tf_op jit(solution)/shard_map/psum | solution.py:69
  68.9 1.9 fusion.28
  70.8 2.4 collective-permute-start
  73.3 2.7 collective-permute-start.1
  76.0 0.6 fusion.48
  79.1 1.4 fusion.49
  80.5 1.8 slice_bitcast_fusion.5
  82.7 2.4 pad_maximum_fusion
  85.1 59.6 %conditional.3 = (f32[1,2,16384]{2,1,0:T(2,128)S(1)}) conditional(s32[]{:T(128)} %convert_element_type.31, () %tuple.29, (bf16[256,2,32,128]{3,0,2,1:T(8,128)(2,1)}, bf16[256,32,128]{2,0,1:T(8,128)(2,1)S(1)}, f32[2,512]{1,0:T(2,128)S(1)}) %tuple.30), branch_computations={%region_3.4_spmd, %region_4.5_spmd} | conditional | flops 738197504 | bytes 73535496 | solution.py:88
  85.1 16.0 %fusion.6 = f32[256,2,128,128]{3,2,1,0:T(8,128)} fusion(bf16[256,2,32,128]{3,0,2,1:T(8,128)(2,1)} %get-tuple-element.89, bf16[256,32,128,1]{2,0,1,3:T(8,128)(2,1)S(1)} %bitcast.162), kind=kOutput, calls=%fused_computation.4 | convolution fusion | flops 536870912 | bytes 39845888 | tf_op jit(solution)/shard_map/cond/branch_1_fun/fkwi,fwj->fkij/dot_general | solution.py:38
  101.1 43.1 %fusion.3 = f32[1,2,16384]{2,1,0:T(2,128)S(1)} fusion(f32[2,512]{1,0:T(2,128)S(1)} %get-tuple-element.37, f32[64,8,128,128]{3,2,1,0:T(8,128)} %bitcast.157), kind=kOutput, calls=%fused_computation.3 | convolution fusion | flops 201326592 | bytes 33689600 | tf_op jit(solution)/shard_map/cond/branch_1_fun/dot_general | solution.py:42
  144.8 1.8 slice_bitcast_fusion.3
  146.6 1.5 pad_maximum_fusion.2
  148.1 1.8 slice_bitcast_fusion.1
  150.1 59.2 %conditional.4 = (f32[1,2,16384]{2,1,0:T(2,128)S(1)}) conditional(s32[]{:T(128)} %convert_element_type.38, () %tuple.31, (bf16[256,2,32,128]{3,0,2,1:T(8,128)(2,1)}, bf16[256,32,128]{2,0,1:T(8,128)(2,1)}, f32[2,512]{1,0:T(2,128)S(1)}) %tuple.32), branch_computations={%region_5.6_spmd, %region_6.7_spmd} | conditional | flops 738197504 | bytes 73535496 | solution.py:88
  150.1 16.0 %fusion.15 = f32[256,2,128,128]{3,2,1,0:T(8,128)} fusion(bf16[256,2,32,128]{3,0,2,1:T(8,128)(2,1)} %get-tuple-element.92, bf16[256,32,128,1]{2,0,1,3:T(8,128)(2,1)} %bitcast.161), kind=kOutput, calls=%fused_computation.11 | convolution fusion | flops 536870912 | bytes 39845888 | tf_op jit(solution)/shard_map/cond/branch_1_fun/fkwi,fwj->fkij/dot_general | solution.py:38
  166.1 42.9 %fusion.12 = f32[1,2,16384]{2,1,0:T(2,128)S(1)} fusion(f32[2,512]{1,0:T(2,128)S(1)} %get-tuple-element.40, f32[64,8,128,128]{3,2,1,0:T(8,128)} %bitcast.158), kind=kOutput, calls=%fused_computation.10 | convolution fusion | flops 201326592 | bytes 33689600 | tf_op jit(solution)/shard_map/cond/branch_1_fun/dot_general | solution.py:42
  209.3 59.3 %conditional.5 = (f32[1,2,16384]{2,1,0:T(2,128)S(1)}) conditional(s32[]{:T(128)} %convert_element_type.39, () %tuple.33, (bf16[256,2,32,128]{3,0,2,1:T(8,128)(2,1)}, bf16[256,32,128]{2,0,1:T(8,128)(2,1)S(1)}, f32[2,512]{1,0:T(2,128)S(1)}) %tuple.34), branch_computations={%region_7.8_spmd, %region_8.9_spmd} | conditional | flops 738197504 | bytes 73535496 | solution.py:88
  209.3 16.0 %fusion.24 = f32[256,2,128,128]{3,2,1,0:T(8,128)} fusion(bf16[256,2,32,128]{3,0,2,1:T(8,128)(2,1)} %get-tuple-element.95, bf16[256,32,128,1]{2,0,1,3:T(8,128)(2,1)S(1)} %bitcast.160), kind=kOutput, calls=%fused_computation.18 | convolution fusion | flops 536870912 | bytes 39845888 | tf_op jit(solution)/shard_map/cond/branch_1_fun/fkwi,fwj->fkij/dot_general | solution.py:38
  225.3 43.0 %fusion.21 = f32[1,2,16384]{2,1,0:T(2,128)S(1)} fusion(f32[2,512]{1,0:T(2,128)S(1)} %get-tuple-element.43, f32[64,8,128,128]{3,2,1,0:T(8,128)} %bitcast.159), kind=kOutput, calls=%fused_computation.17 | convolution fusion | flops 201326592 | bytes 33689600 | tf_op jit(solution)/shard_map/cond/branch_1_fun/dot_general | solution.py:42
  268.6 0.9 pad_maximum_fusion.4
  269.6 0.6 dynamic-slice
  270.2 25.0 %all-reduce.3.cloned.1.call-done = f32[3,2,16384]{2,1,0:T(2,128)} async-done(((f32[3,2,16384]{2,1,0:T(2,128)}), f32[3,2,16384]{2,1,0:T(2,128)}) %all-reduce.3.cloned.1.call-update) | async-done | bytes 393232
  295.1 1.9 constant_dynamic-slice_fusion.2
  297.0 3.4 %collective-permute-start.2 = (f32[1,16384]{1,0:T(1,128)S(1)}, f32[1,16384]{1,0:T(1,128)S(1)}, u32[]{:S(2)}, u32[]{:S(2)}) collective-permute-start(f32[1,16384]{1,0:T(1,128)S(1)} %bitcast.166), channel_id=1, source_target_pairs={{0,4},{2,6},{4,8},{6,10},{8,12},{10,14},{12,16},{14,18},{16,20},{1... | collective-permute-start | bytes 196616 | tf_op jit(solution)/shard_map/ppermute | solution.py:17
  300.4 1.9 collective-permute-start.3
  302.6 1.4 collective-permute-done.2
  304.1 2.8 collective-permute-done.3
  306.9 0.9 copy.94
  (43 shorter events, 3.0 us)
Async XLA Ops:
  6.5 288.6 %all-reduce.3.cloned.1.call-start = ((), (), s32[]{:S(2)}) async-start(), calls=%async_computation.1 | async-start | bytes 786432
  68.9 7.0 %copy-start = (s32[16]{0:T(128)S(1)}, s32[16]{0:T(128)}, u32[]{:S(2)}) copy-start(s32[16]{0:T(128)} %param.11) | copy-start | bytes 196
  70.8 73.9 %collective-permute-start = (bf16[2,256,16,128]{3,1,0,2:T(8,128)(2,1)}, bf16[2,256,16,128]{3,1,0,2:T(8,128)(2,1)}, u32[]{:S(2)}, u32[]{:S(2)}) collective-permute-start(bf16[2,256,16,128]{3,1,0,2:T(8,128)(2,1)} %fusion.28), channel_id=1, source_target_pairs={{2,0},{4,2},{6,4},{8,6},{10,8},{12,10},{14,12},{16,14},{18,16},{20... | collective-permute-start | bytes 6291464 | tf_op jit(solution)/shard_map/ppermute | solution.py:17
  73.3 74.8 %collective-permute-start.1 = (bf16[2,256,16,128]{3,1,0,2:T(8,128)(2,1)}, bf16[2,256,16,128]{3,1,0,2:T(8,128)(2,1)}, u32[]{:S(2)}, u32[]{:S(2)}) collective-permute-start(bf16[2,256,16,128]{3,1,0,2:T(8,128)(2,1)} %fusion.28), channel_id=1, source_target_pairs={{4,0},{6,2},{8,4},{10,6},{12,8},{14,10},{16,12},{18,14},{20,16},{2... | collective-permute-start | bytes 6291464 | tf_op jit(solution)/shard_map/ppermute | solution.py:17
  209.3 60.3 %copy-start.1 = (u32[32]{0:T(128)S(1)}, u32[32]{0:T(128)}, u32[]{:S(2)}) copy-start(u32[32]{0:T(128)} %constant.41) | copy-start | bytes 388
  297.0 7.1 %collective-permute-start.2 = (f32[1,16384]{1,0:T(1,128)S(1)}, f32[1,16384]{1,0:T(1,128)S(1)}, u32[]{:S(2)}, u32[]{:S(2)}) collective-permute-start(f32[1,16384]{1,0:T(1,128)S(1)} %bitcast.166), channel_id=1, source_target_pairs={{0,4},{2,6},{4,8},{6,10},{8,12},{10,14},{12,16},{14,18},{16,20},{1... | collective-permute-start | bytes 196616 | tf_op jit(solution)/shard_map/ppermute | solution.py:17
  300.4 6.5 %collective-permute-start.3 = (f32[1,16384]{1,0:T(1,128)S(1)}, f32[1,16384]{1,0:T(1,128)S(1)}, u32[]{:S(2)}, u32[]{:S(2)}) collective-permute-start(f32[1,16384]{1,0:T(1,128)S(1)} %bitcast.164), channel_id=1, source_target_pairs={{0,2},{2,4},{4,6},{6,8},{8,10},{10,12},{12,14},{14,16},{16,18},{18... | collective-permute-start | bytes 196616 | tf_op jit(solution)/shard_map/ppermute | solution.py:17
Sparse Core Ops, SparseCore 0:
  269.7 25.3 all-reduce.2
